TPU v7x, 512 devices: a whole 4x8x8 slice. The times are simulated.
512 devices in a mesh: cam: 16 (over x_lo, y), space: 32 (over x_hi, z, core).
Axes of the slice: x: 4 (x_hi: 2, x_lo: 2; x = x_hi * 2 + x_lo), y: 8, z: 8, core: 2. Of those that a mesh axis runs over, the one named last changes fastest.
Arguments:
- features: float32 [64, 131072], P(None, ('cam', 'space')), may hold values from -6 to 6
- positions: float32 [3, 131072], P(None, ('cam', 'space')), may hold values from -6144 to 6144, as said below
- spreads: float32 [131072], P(('cam', 'space')), may hold values from 16 to 64
- logits: float32 [131072], P(('cam', 'space')), may hold values from -6 to -2
- camera: float32 [16, 3], replicated, may hold values from -1 to 1
- decoder: bfloat16 [64, 512], replicated, may hold values from -0.75 to 0.75
- tile_lists: int32 [16, 32, 16, 256], P('cam', 'space'), may hold values from 0 to 8191, as said below
- counts: int32 [16, 32, 16], P('cam', 'space'), may hold values from 1 to 256, as said below
- targets: bfloat16 [16, 32, 16, 256, 512], P('cam', 'space'), may hold values from -6 to 6
Outputs:
- grad_features: float32 [64, 131072], P(None, ('cam', 'space'))
- grad_logits: float32 [131072], P(('cam', 'space'))
Inputs may be any that keep to these rules, and one draw needn't show every extreme that they name: `positions`: rows are x, y and depth; depth lies between 4 and 8. `tile_lists`: the list of tile (c, s, j) names only ids j * 256 + q or 4096 + j * 256 + q with 0 <= q < 256, no id twice; lists of tile row 0 name only ids below 4096. `counts`: some tile has all 256 entries live.
All inputs are finite; a program needn't handle non-finite values.
Results may differ from a plain program's by a relative error of at most 0.003.
Values may be sent and summed in bfloat16 or wider, within the bound.
No kernel may reach another device: no remote copies, remote signals or barrier semaphores. Data moves between devices by JAX's collectives and lax.ppermute only.
A program may use at most 64 MiB of HBM per device.

v0:
```python
import jax
import jax.numpy as jnp
from jax import lax
from jax.sharding import PartitionSpec as P

TS = 16


def shifted(shard, axis, by):
    length = lax.axis_size(axis)
    pairs = [(i, i + by) for i in range(length) if 0 <= i + by < length]
    return lax.ppermute(shard, axis, pairs)


def project_terms(
    gathered, viewers, tile_row, columns, live_counts, grad_maker, image_width, image_height
):
    channels = gathered.shape[0] - 5
    tiles_here = gathered.shape[1]
    length = gathered.shape[2]
    step_len = 128
    block_count = length // step_len
    pixel_count = TS * TS
    feature_bf = gathered[:channels].astype(jnp.bfloat16)
    distance = gathered[channels + 2] - 0.05 * viewers[:, 2:3]
    centre_u = (gathered[channels] - 0.75 * TS * viewers[:, 0:1]) / distance + 0.5 * image_width
    centre_v = (
        gathered[channels + 1] - 0.75 * TS * viewers[:, 1:2]
    ) / distance + 0.5 * image_height
    radius = gathered[channels + 3] / distance
    sigmoid_open = jax.nn.sigmoid(gathered[channels + 4])
    opacity = 0.99 * sigmoid_open
    sigmoid_slope = 0.99 * sigmoid_open * (1.0 - sigmoid_open)
    pixel_id = jnp.arange(pixel_count, dtype=jnp.int32)
    pixel_u = (columns[:, None] * TS + pixel_id[None, :] % TS).astype(jnp.float32) + 0.5
    pixel_v = (tile_row * TS + pixel_id // TS).astype(jnp.float32) + 0.5
    alive_mask = (jnp.arange(length, dtype=jnp.int32)[None, :] < live_counts[:, None]).astype(
        jnp.float32
    )
    logit_gate_all = alive_mask * sigmoid_slope
    steps_used = (jnp.max(live_counts) + step_len - 1) // step_len

    def block_terms(first_entry):

        def window_of(source_array):
            return lax.dynamic_slice_in_dim(
                source_array, first_entry, step_len, axis=source_array.ndim - 1
            )

        delta_u = pixel_u[:, :, None] - window_of(centre_u)[:, None, :]
        delta_v = pixel_v[None, :, None] - window_of(centre_v)[:, None, :]
        spread = window_of(radius)[:, None, :]
        falloff = jnp.exp(-(delta_u * delta_u + delta_v * delta_v) / (2.0 * spread * spread))
        opaque = (window_of(opacity) * window_of(alive_mask))[:, None, :] * falloff
        log_keep = jnp.log(1.0 - opaque)
        inner_log = jnp.cumsum(log_keep, axis=2) - log_keep
        return (
            falloff,
            opaque,
            log_keep,
            inner_log,
            window_of(feature_bf),
            window_of(logit_gate_all),
        )

    def forward(position, state_in):
        log_start, feature_sum, starts = state_in
        first_entry = position * step_len
        falloff, opaque, log_keep, inner_log, block_feat, unused = block_terms(first_entry)
        weight = opaque * jnp.exp(log_start[:, :, None] + inner_log)
        feature_sum = feature_sum + jnp.einsum(
            "tpk,ctk->tcp",
            weight.astype(jnp.bfloat16),
            block_feat,
            preferred_element_type=jnp.float32,
        )
        starts = lax.dynamic_update_index_in_dim(starts, log_start, position, 0)
        return (log_start + jnp.sum(log_keep, axis=2), feature_sum, starts)

    initial = (
        jnp.zeros((tiles_here, pixel_count), jnp.float32),
        jnp.zeros((tiles_here, channels, pixel_count), jnp.float32),
        jnp.zeros((block_count, tiles_here, pixel_count), jnp.float32),
    )
    unused_log, feature_sum, starts = lax.fori_loop(0, steps_used, forward, initial)
    composite = feature_sum.astype(jnp.bfloat16)
    pixel_grad = grad_maker(composite).astype(jnp.bfloat16)

    def backward(reverse_turn, state_in):
        behind_sum, feature_grad, logit_grad = state_in
        position = steps_used - 1 - reverse_turn
        first_entry = position * step_len
        falloff, opaque, log_keep, inner_log, block_feat, logit_gate = block_terms(first_entry)
        keep_to = jnp.exp(
            lax.dynamic_index_in_dim(starts, position, 0, keepdims=False)[:, :, None] + inner_log
        )
        weight = opaque * keep_to
        weight_bf = weight.astype(jnp.bfloat16)
        contrib = jnp.einsum(
            "tcp,ctk->tpk", pixel_grad, block_feat, preferred_element_type=jnp.float32
        )
        weighted = weight * contrib
        block_total = jnp.sum(weighted, axis=2)
        behind = behind_sum[:, :, None] + block_total[:, :, None] - jnp.cumsum(weighted, axis=2)
        dopaque = keep_to * contrib - behind / (1.0 - opaque)
        logit_part = logit_gate * jnp.sum(dopaque * falloff, axis=1)
        feature_part = jnp.einsum(
            "tpk,tcp->ctk", weight_bf, pixel_grad, preferred_element_type=jnp.float32
        )
        feature_grad = lax.dynamic_update_slice_in_dim(
            feature_grad, feature_part, first_entry, axis=2
        )
        logit_grad = lax.dynamic_update_slice_in_dim(logit_grad, logit_part, first_entry, axis=1)
        return (behind_sum + block_total, feature_grad, logit_grad)

    initial_back = (
        jnp.zeros((tiles_here, pixel_count), jnp.float32),
        jnp.zeros((channels, tiles_here, length), jnp.float32),
        jnp.zeros((tiles_here, length), jnp.float32),
    )
    unused_behind, feature_grad, logit_grad = lax.fori_loop(0, steps_used, backward, initial_back)
    return (feature_grad, logit_grad)


def full_target_rule(pixel_targets, decoder):
    decoder_wide = decoder.astype(jnp.float32)

    def make_grad(composite):
        decoded = jnp.einsum("tcp,cd->tpd", composite, decoder, preferred_element_type=jnp.float32)
        residual = decoded - pixel_targets.astype(jnp.float32)
        return jnp.einsum("tpd,cd->tcp", residual, decoder_wide, precision=lax.Precision.HIGHEST)

    return make_grad


def on_device(features, positions, spreads, logits, camera, decoder, tile_lists, counts, targets):
    channels = features.shape[0]
    length = features.shape[1]
    camera_count = lax.axis_size("cam")
    space_count = lax.axis_size("space")
    camera_id = lax.axis_index("cam")
    tile_row = lax.axis_index("space")
    image_width = TS * camera_count
    image_height = TS * space_count
    block_rows = camera_count * length
    own_slab = jnp.concatenate([features, positions, spreads[None], logits[None]], axis=0)
    upper_slab = shifted(own_slab, "space", 1)
    both_slabs = lax.all_gather(jnp.stack([own_slab, upper_slab]), "cam", axis=2, tiled=True)
    gauss_table = jnp.concatenate([both_slabs[0], both_slabs[1]], axis=1)
    entries = tile_lists[0, 0]
    picker = (jnp.arange(camera_count, dtype=jnp.int32) == camera_id).astype(jnp.float32)
    viewers = jnp.broadcast_to(jnp.sum(camera * picker[:, None], axis=0), (camera_count, 3))
    columns = jnp.arange(camera_count, dtype=jnp.int32)
    gathered = jnp.take(gauss_table, entries, axis=1)
    grad_maker = full_target_rule(targets[0, 0], decoder)
    feature_grad, logit_grad = project_terms(
        gathered, viewers, tile_row, columns, counts[0, 0], grad_maker, image_width, image_height
    )
    values = jnp.concatenate([feature_grad, logit_grad[None]], axis=0)
    totals = jnp.zeros((channels + 1, 2 * block_rows), jnp.float32).at[:, entries].add(values)
    returned = shifted(totals[:, block_rows:], "space", -1)
    summed = lax.psum_scatter(
        totals[:, :block_rows] + returned, "cam", scatter_dimension=1, tiled=True
    )
    return (summed[:channels], summed[channels])


def solution(mesh):
    placed = (
        P(None, ("cam", "space")),
        P(None, ("cam", "space")),
        P(("cam", "space")),
        P(("cam", "space")),
        P(),
        P(),
        P("cam", "space", None, None),
        P("cam", "space", None),
        P("cam", "space", None, None, None),
    )
    return jax.shard_map(
        on_device,
        mesh=mesh,
        in_specs=placed,
        out_specs=(P(None, ("cam", "space")), P(("cam", "space"))),
        check_vma=False,
    )
```

profile of v0, /device:TPU:4, one launch (start us, length us, event | category | flops | bytes accessed | tf_op | source)
XLA Modules:
  0.0 300.1 jit_solution(15788181093214662596)
XLA Ops:
  10.8 1.9 collective-permute-start
  12.9 10.9 %collective-permute-done = f32[69,256]{0,1:T(8,128)S(1)} collective-permute-done((f32[69,256]{0,1:T(8,128)S(1)}, f32[69,256]{0,1:T(8,128)S(1)}, u32[]{:S(2)}, u32[]{:S(2)}) %collective-permute-start) | collective-permute-done | bytes 70688 | tf_op jit(solution)/shard_map/ppermute | solution.py:12
  28.9 72.8 %all-gather.2.cloned.1.call-done = f32[2,69,4096]{1,2,0:T(8,128)} async-done(((f32[2,69,256]{1,2,0:T(8,128)}), f32[2,69,4096]{1,2,0:T(8,128)}) %all-gather.2.cloned.1.call-update) | async-done | bytes 2261008 | tf_op jit(solution)/shard_map/all_gather | solution.py:148
  101.7 2.5 slice_bitcast_fusion.1
  104.2 2.2 pad_maximum_fusion
  106.4 13.0 %gather_fusion = f32[4096,69]{1,0:T(8,128)S(1)} fusion(f32[69,8192]{0,1:T(8,128)} %pad_maximum_fusion, s32[4096]{0:T(1024)S(1)} %broadcast_clamp_fusion), kind=kCustom, calls=%fused_computation | custom fusion | bytes 2277376 | tf_op jit(solution)/shard_map/jit(_take)/gather | solution.py:154
  121.0 11.3 %while.32 = (s32[]{:T(128)}, f32[16,256]{1,0:T(8,128)S(1)}, f32[16,64,256]{2,1,0:T(8,128)S(1)}, f32[2,16,256]{2,1,0:T(8,128)S(1)}, s32[]{:T(128)}, /*index=5*/f3...) while((s32[]{:T(128)}, f32[16,256]{1,0:T(8,128)S(1)}, ...), condition=%wide.region_5.6_spmd.clone, body=%wide.region_2.5_spmd.clone.sunk | while | flops 150754048 | bytes 4895069 | solution.py:85
  121.7 1.5 fusion.84
  123.1 2.8 multiply_convert_fusion.2
  127.2 1.5 fusion.84
  128.7 2.8 multiply_convert_fusion.2
  132.3 1.3 fusion.44
  134.4 4.9 %fusion.43 = bf16[16,64,256]{2,1,0:T(8,128)(2,1)S(1)} fusion(f32[16,256,512]{2,1,0:T(8,128)S(1)} %fusion.44, bf16[1,1,16,256,512]{4,3,2,1,0:T(8,128)(2,1)S(1)} %copy-done.1, bf16[64,512]{1,0:T(8,128)(2,1)S(1)} %copy-done), kind=kOutput, calls=%fused_computation.78 | convolution fusion | flops 1615069184 | bytes 13172736 | tf_op jit(solution)/shard_map/tpd,cd->tcp/dot_general | solution.py:131
  139.4 25.9 %while.33 = (s32[]{:T(128)}, f32[16,256]{1,0:T(8,128)S(1)}, f32[64,16,256]{2,0,1:T(8,128)S(1)}, f32[16,256]{1,0:T(8,128)S(1)}, s32[]{:T(128)}, /*index=5*/s32[]{...) while((s32[]{:T(128)}, f32[16,256]{1,0:T(8,128)S(1)}, ...), condition=%wide.region_11.12_spmd.clone, body=%wide.region_6.11_spmd.clone.sunk | while | flops 295195392 | bytes 27490700 | solution.py:121
  141.0 1.3 fusion.91
  142.3 2.2 fusion.93
  144.5 2.5 fusion.92
  147.0 1.3 fusion.94
  148.2 4.2 %fusion.95 = f32[16,128]{1,0:T(8,128)S(1)} fusion(f32[16,128,256]{2,1,0:T(8,128)S(1)} %get-tuple-element.746, f32[16,256,128]{1,0,2:T(8,128)S(1)} %fusion.94, f32[16,256]{1,0:T(8,128)S(1)} %add.491, f32[16,128]{1,0:T(8,128)S(1)} %get-tuple-element.741, f32[16,128]{1,0:T(8,128)S(1)} %get-tuple-element.742, f32[256]{0:T(256)S(1)} %fusion.90, ...), kind=kLoop, calls=%fused_computation.35.clone.1 | loop fusion | flops 8910848 | bytes 6382592 | tf_op jit(solution)/shard_map/while/body/reduce_sum | solution.py:106
  155.1 2.2 fusion.93
  157.3 2.5 fusion.92
  159.8 1.3 fusion.94
  161.1 4.2 %fusion.95 = f32[16,128]{1,0:T(8,128)S(1)} fusion(f32[16,128,256]{2,1,0:T(8,128)S(1)} %get-tuple-element.746, f32[16,256,128]{1,0,2:T(8,128)S(1)} %fusion.94, f32[16,256]{1,0:T(8,128)S(1)} %add.491, f32[16,128]{1,0:T(8,128)S(1)} %get-tuple-element.741, f32[16,128]{1,0:T(8,128)S(1)} %get-tuple-element.742, f32[256]{0:T(256)S(1)} %fusion.90, ...), kind=kLoop, calls=%fused_computation.35.clone.1 | loop fusion | flops 8910848 | bytes 6382592 | tf_op jit(solution)/shard_map/while/body/reduce_sum | solution.py:106
  166.3 24.5 %scatter_custom_fusion = f32[65,8192]{0,1:T(8,128)} fusion(s32[4096]{0:T(1024)S(1)} %bitcast.99, f32[4096,65]{1,0:T(8,128)S(1)} %bitcast.95, f32[]{:T(128)} %constant.142.clone.1), kind=kCustom, calls=%fused_computation.75 | custom fusion | flops 266240 | bytes 2129924 | tf_op jit(solution)/shard_map/scatter-add | solution.py:160
  190.8 1.6 slice-done
  193.3 1.9 collective-permute-start.1
  195.2 13.7 %collective-permute-done.1 = f32[65,4096]{1,0:T(8,128)} collective-permute-done((f32[65,4096]{1,0:T(8,128)S(1)}, f32[65,4096]{1,0:T(8,128)}, u32[]{:S(2)}, u32[]{:S(2)}) %collective-permute-start.1) | collective-permute-done | bytes 1064992 | tf_op jit(solution)/shard_map/ppermute | solution.py:12
  208.9 1.8 copy.73
  210.7 3.1 %slice_add_fusion = f32[65,4096]{0,1:T(8,128)} fusion(f32[65,4096]{0,1:T(8,128)S(1)} %copy.73, f32[65,8192]{0,1:T(8,128)} %scatter_custom_fusion), kind=kLoop, calls=%fused_computation.72 | loop fusion | flops 266240 | bytes 3194880 | tf_op jit(solution)/shard_map/add | solution.py:163
  213.9 76.1 %reduce-scatter.2.cloned.1.call-done = f32[65,256]{0,1:T(8,128)} async-done(((f32[65,4096]{0,1:T(8,128)}), f32[65,256]{0,1:T(8,128)}) %reduce-scatter.2.cloned.1.call-update) | async-done | bytes 66576 | tf_op jit(solution)/shard_map/reduce_scatter | solution.py:162
  290.0 1.6 copy.74
  291.6 1.7 slice_reduce_fusion
  (96 shorter events, 16.7 us)
Async XLA Ops:
  7.2 125.1 %copy-start = (bf16[64,512]{1,0:T(8,128)(2,1)S(1)}, bf16[64,512]{1,0:T(8,128)(2,1)}, u32[]{:S(2)}) copy-start(bf16[64,512]{1,0:T(8,128)(2,1)} %param.18) | copy-start | bytes 196612
  7.2 17.4 %copy-start.3 = (s32[1,1,16]{2,1,0:T(1,128)S(1)}, s32[1,1,16]{2,1,0:T(1,128)}, u32[]{:S(2)}) copy-start(s32[1,1,16]{2,1,0:T(1,128)} %param.20) | copy-start | bytes 196
  7.2 18.7 %copy-start.4 = (f32[16,3]{0,1:T(4,128)S(1)}, f32[16,3]{0,1:T(4,128)}, u32[]{:S(2)}) copy-start(f32[16,3]{0,1:T(4,128)} %param.17) | copy-start | bytes 580
  7.2 20.9 %copy-start.2 = (s32[1,1,16,256]{3,2,1,0:T(8,128)S(1)}, s32[1,1,16,256]{3,2,1,0:T(8,128)}, u32[]{:S(2)}) copy-start(s32[1,1,16,256]{3,2,1,0:T(8,128)} %param.19) | copy-start | bytes 49156
  7.2 94.5 %all-gather.2.cloned.1.call-start = ((), (), s32[]{:S(2)}) async-start(), calls=%async_computation.1 | async-start | bytes 4456448 | tf_op jit(solution)/shard_map/all_gather | solution.py:148
  10.8 13.0 %collective-permute-start = (f32[69,256]{0,1:T(8,128)S(1)}, f32[69,256]{0,1:T(8,128)S(1)}, u32[]{:S(2)}, u32[]{:S(2)}) collective-permute-start(f32[69,256]{0,1:T(8,128)S(1)} %pad_maximum_fusion.2), channel_id=1, source_target_pairs={{0,1},{1,2},{2,3},{3,4},{4,5},{5,6},{6,7},{7,8},{8,9},{9,10},{10,1... | collective-permute-start | bytes 211976 | tf_op jit(solution)/shard_map/ppermute | solution.py:12
  24.5 265.5 %reduce-scatter.2.cloned.1.call-start = ((), (), s32[]{:S(2)}) async-start(), calls=%async_computation.2 | async-start | bytes 2228224 | tf_op jit(solution)/shard_map/reduce_scatter | solution.py:162
  132.2 2.2 copy-start.1
  190.8 1.6 slice-start
  193.3 15.6 %collective-permute-start.1 = (f32[65,4096]{1,0:T(8,128)S(1)}, f32[65,4096]{1,0:T(8,128)}, u32[]{:S(2)}, u32[]{:S(2)}) collective-permute-start(f32[65,4096]{1,0:T(8,128)S(1)} %copy.72), channel_id=1, source_target_pairs={{1,0},{2,1},{3,2},{4,3},{5,4},{6,5},{7,6},{8,7},{9,8},{10,9},{11,1... | collective-permute-start | bytes 3194888 | tf_op jit(solution)/shard_map/ppermute | solution.py:12
Sparse Core Ops, SparseCore 0:
  24.7 76.9 all-gather.1
  214.0 75.9 reduce-scatter.1
where the time goes:
time: 301 us; the launch traced here: 300 us
  waiting for transfers between devices  174 us (58%)
  other arithmetic  56.9 us (19%)
  local copies, waits for them, and re-layouts  31.3 us (10%)
  between operations  17.1 us (6%)
  matrix products  16.6 us (6%)
  starting transfers between devices  3.92 us (1%)
    reduce_scatter x1, waiting for transfers between devices, on_device(): lax.psum_scatter(totals[:, :block_rows] + returned, 'cam', scatter_dimens...  76.1 us
    all_gather x1, waiting for transfers between devices, on_device(): lax.all_gather(jnp.stack([own_slab, upper_slab]), 'cam', axis=2, tiled=True)  72.8 us
    ppermute x2, waiting for transfers between devices, shifted(): return lax.ppermute(shard, axis, pairs)  24.6 us
    scatter-add x1, other arithmetic, on_device(): jnp.zeros((channels + 1, 2 * block_rows), jnp.float32).at[:, entries]  24.5 us
    gather x2, local copies, waits for them, and re-layouts, on_device(): gathered = jnp.take(gauss_table, entries, axis=1)  14 us
    reduce_sum x2, other arithmetic, backward(): logit_part = logit_gate * jnp.sum(dopaque * falloff, axis=1)  8.48 us
    another operation x4, other arithmetic, block_terms(): inner_log = jnp.cumsum(log_keep, axis=2) - log_keep  8.17 us
  transfers between devices with their start and end apart: 4, of which 4 were waited for; matrix products, arithmetic and copies ran while one was open for 1% of the time, Pallas kernels for 0%

commit v1 on v0

--- a/solution.py
+++ b/solution.py
@@ -145,7 +145,11 @@
     block_rows = camera_count * length
     own_slab = jnp.concatenate([features, positions, spreads[None], logits[None]], axis=0)
     upper_slab = shifted(own_slab, "space", 1)
-    both_slabs = lax.all_gather(jnp.stack([own_slab, upper_slab]), "cam", axis=2, tiled=True)
+    arr_in = jnp.stack([own_slab, upper_slab])
+    both_slabs = jnp.concatenate(
+        jax.lax.all_to_all(jnp.stack(jax.lax.axis_size("cam") * [arr_in], axis=0), "cam", 0, 0),
+        axis=2,
+    )
     gauss_table = jnp.concatenate([both_slabs[0], both_slabs[1]], axis=1)
     entries = tile_lists[0, 0]
     picker = (jnp.arange(camera_count, dtype=jnp.int32) == camera_id).astype(jnp.float32)

time: 301 us -> 289 us (0.960)
  waiting for transfers between devices: 174 us -> 145 us
  starting transfers between devices: 3.92 us -> 16 us
  local copies, waits for them, and re-layouts: 31.3 us -> 35.2 us
    all_gather x1 -> x0, waiting for transfers between devices: 72.8 us -> none  [on_device(): lax.all_gather(jnp.stack([own_slab, upper_slab]), 'cam', axis=2, tiled=True)]
    all_to_all x0 -> x1, waiting for transfers between devices: none -> 41.9 us  [on_device(): jax.lax.all_to_all(jnp.stack(jax.lax.axis_size('cam') * [arr_in], axis=0)...]
    all_to_all x0 -> x1, starting transfers between devices: none -> 8.87 us  [on_device(): jax.lax.all_to_all(jnp.stack(jax.lax.axis_size('cam') * [arr_in], axis=0)...]
    slice x0 -> x3, local copies, waits for them, and re-layouts: none -> 7.67 us  [on_device(): gauss_table = jnp.concatenate([both_slabs[0], both_slabs[1]], axis=1)]
    ppermute x2, starting transfers between devices: 3.84 us -> 7.11 us  [shifted(): return lax.ppermute(shard, axis, pairs)]
where the time goes in v1:
time: 289 us
  waiting for transfers between devices  145 us (50%)
  other arithmetic  58.4 us (20%)
  local copies, waits for them, and re-layouts  35.2 us (12%)
  between operations  16.9 us (6%)
  matrix products  16.6 us (6%)
  starting transfers between devices  16 us (6%)
    reduce_scatter x1, waiting for transfers between devices, on_device(): lax.psum_scatter(totals[:, :block_rows] + returned, 'cam', scatter_dimens...  78.8 us
    all_to_all x1, waiting for transfers between devices, on_device(): jax.lax.all_to_all(jnp.stack(jax.lax.axis_size('cam') * [arr_in], axis=0)...  41.9 us
    scatter-add x1, other arithmetic, on_device(): jnp.zeros((channels + 1, 2 * block_rows), jnp.float32).at[:, entries]  24.5 us
    ppermute x2, waiting for transfers between devices, shifted(): return lax.ppermute(shard, axis, pairs)  24.1 us
    gather x2, local copies, waits for them, and re-layouts, on_device(): gathered = jnp.take(gauss_table, entries, axis=1)  14 us
    all_to_all x1, starting transfers between devices, on_device(): jax.lax.all_to_all(jnp.stack(jax.lax.axis_size('cam') * [arr_in], axis=0)...  8.87 us
    reduce_sum x2, other arithmetic, backward(): logit_part = logit_gate * jnp.sum(dopaque * falloff, axis=1)  8.48 us
    another operation x4, other arithmetic, block_terms(): inner_log = jnp.cumsum(log_keep, axis=2) - log_keep  8.17 us
  transfers between devices with their start and end apart: 4, of which 4 were waited for; matrix products, arithmetic and copies ran while one was open for 1% of the time, Pallas kernels for 0%

profile of v1, /device:TPU:4, one launch (start us, length us, event | category | flops | bytes accessed | tf_op | source)
XLA Modules:
  0.0 288.5 jit_solution(18108499151227215452)
XLA Ops:
  8.1 1.9 collective-permute-start
  10.0 10.4 %collective-permute-done = f32[69,256]{1,0:T(8,128)S(1)} collective-permute-done((f32[69,256]{1,0:T(8,128)S(1)}, f32[69,256]{1,0:T(8,128)S(1)}, u32[]{:S(2)}, u32[]{:S(2)}) %collective-permute-start) | collective-permute-done | bytes 70688 | tf_op jit(solution)/shard_map/ppermute | solution.py:12
  20.6 2.0 stack.11
  22.6 8.9 %all-to-all-start = ((f32[16,2,69,256]{3,1,2,0:T(2,128)}), f32[16,2,69,256]{3,1,2,0:T(2,128)S(1)}, u32[]{:S(2)}, u32[]{:S(2)}) async-start(f32[16,2,69,256]{3,1,2,0:T(2,128)} %stack.11), calls=%async_computation | async-start | bytes 4521984 | tf_op jit(solution)/shard_map/all_to_all | solution.py:150
  35.7 41.9 %all-to-all-done = f32[16,2,69,256]{3,1,2,0:T(2,128)S(1)} async-done(((f32[16,2,69,256]{3,1,2,0:T(2,128)}), f32[16,2,69,256]{3,1,2,0:T(2,128)S(1)}, u32[]{:S(2)}, u32[]{:S(2)}) %all-to-all-start) | async-done | bytes 2261024 | tf_op jit(solution)/shard_map/all_to_all | solution.py:150
  77.6 2.7 fusion.63
  80.3 2.6 copy.54
  82.9 2.4 copy.55
  85.2 3.8 %pad_maximum_fusion = f32[69,8192]{0,1:T(8,128)} fusion(f32[69,4096]{0,1:T(8,128)} %bitcast.95, f32[69,4096]{0,1:T(8,128)S(1)} %bitcast.94), kind=kLoop, calls=%fused_computation.70 | loop fusion | flops 565248 | bytes 4521984 | tf_op jit(solution)/shard_map/concatenate | solution.py:153
  89.0 13.0 %gather_fusion = f32[4096,69]{1,0:T(8,128)S(1)} fusion(f32[69,8192]{0,1:T(8,128)} %pad_maximum_fusion, s32[4096]{0:T(1024)S(1)} %broadcast_clamp_fusion), kind=kCustom, calls=%fused_computation | custom fusion | bytes 2277376 | tf_op jit(solution)/shard_map/jit(_take)/gather | solution.py:158
  103.6 11.3 %while.32 = (s32[]{:T(128)}, f32[16,256]{1,0:T(8,128)S(1)}, f32[16,64,256]{2,1,0:T(8,128)S(1)}, f32[2,16,256]{2,1,0:T(8,128)S(1)}, s32[]{:T(128)}, /*index=5*/f3...) while((s32[]{:T(128)}, f32[16,256]{1,0:T(8,128)S(1)}, ...), condition=%wide.region_5.6_spmd.clone, body=%wide.region_2.5_spmd.clone.sunk | while | flops 150754048 | bytes 4895069 | solution.py:85
  104.3 1.5 fusion.85
  105.8 2.8 multiply_convert_fusion.2
  109.8 1.5 fusion.85
  111.3 2.8 multiply_convert_fusion.2
  117.1 4.9 %fusion.43 = bf16[16,64,256]{2,1,0:T(8,128)(2,1)S(1)} fusion(f32[16,256,512]{2,1,0:T(8,128)S(1)} %fusion.44, bf16[1,1,16,256,512]{4,3,2,1,0:T(8,128)(2,1)S(1)} %copy-done.1, bf16[64,512]{1,0:T(8,128)(2,1)S(1)} %copy-done), kind=kOutput, calls=%fused_computation.76 | convolution fusion | flops 1615069184 | bytes 13172736 | tf_op jit(solution)/shard_map/tpd,cd->tcp/dot_general | solution.py:131
  122.1 25.7 %while.33 = (s32[]{:T(128)}, f32[16,256]{1,0:T(8,128)S(1)}, f32[64,16,256]{2,0,1:T(8,128)S(1)}, f32[16,256]{1,0:T(8,128)S(1)}, s32[]{:T(128)}, /*index=5*/s32[]{...) while((s32[]{:T(128)}, f32[16,256]{1,0:T(8,128)S(1)}, ...), condition=%wide.region_11.12_spmd.clone, body=%wide.region_6.11_spmd.clone.sunk | while | flops 295195392 | bytes 27490700 | solution.py:121
  124.7 2.2 fusion.94
  126.9 2.5 fusion.93
  130.7 4.2 %fusion.96 = f32[16,128]{1,0:T(8,128)S(1)} fusion(f32[16,128,256]{2,1,0:T(8,128)S(1)} %get-tuple-element.748, f32[16,256,128]{1,0,2:T(8,128)S(1)} %fusion.95, f32[16,256]{1,0:T(8,128)S(1)} %add.491, f32[16,128]{1,0:T(8,128)S(1)} %get-tuple-element.743, f32[16,128]{1,0:T(8,128)S(1)} %get-tuple-element.744, f32[256]{0:T(256)S(1)} %fusion.91, ...), kind=kLoop, calls=%fused_computation.35.clone.1 | loop fusion | flops 8910848 | bytes 6382592 | tf_op jit(solution)/shard_map/while/body/reduce_sum | solution.py:106
  137.5 2.2 fusion.94
  139.7 2.5 fusion.93
  143.5 4.2 %fusion.96 = f32[16,128]{1,0:T(8,128)S(1)} fusion(f32[16,128,256]{2,1,0:T(8,128)S(1)} %get-tuple-element.748, f32[16,256,128]{1,0,2:T(8,128)S(1)} %fusion.95, f32[16,256]{1,0:T(8,128)S(1)} %add.491, f32[16,128]{1,0:T(8,128)S(1)} %get-tuple-element.743, f32[16,128]{1,0:T(8,128)S(1)} %get-tuple-element.744, f32[256]{0:T(256)S(1)} %fusion.91, ...), kind=kLoop, calls=%fused_computation.35.clone.1 | loop fusion | flops 8910848 | bytes 6382592 | tf_op jit(solution)/shard_map/while/body/reduce_sum | solution.py:106
  148.8 24.5 %scatter_custom_fusion = f32[65,8192]{0,1:T(8,128)} fusion(s32[4096]{0:T(1024)S(1)} %bitcast.101, f32[4096,65]{1,0:T(8,128)S(1)} %bitcast.97, f32[]{:T(128)} %constant.142.clone.1), kind=kCustom, calls=%fused_computation.73 | custom fusion | flops 266240 | bytes 2129924 | tf_op jit(solution)/shard_map/scatter-add | solution.py:164
  173.3 1.6 slice-done
  175.7 5.2 %collective-permute-start.1 = (f32[65,4096]{1,0:T(8,128)S(1)}, f32[65,4096]{1,0:T(8,128)}, u32[]{:S(2)}, u32[]{:S(2)}) collective-permute-start(f32[65,4096]{1,0:T(8,128)S(1)} %copy.67), channel_id=1, source_target_pairs={{1,0},{2,1},{3,2},{4,3},{5,4},{6,5},{7,6},{8,7},{9,8},{10,9},{11,1... | collective-permute-start | bytes 3194888 | tf_op jit(solution)/shard_map/ppermute | solution.py:12
  180.9 13.7 %collective-permute-done.1 = f32[65,4096]{1,0:T(8,128)} collective-permute-done((f32[65,4096]{1,0:T(8,128)S(1)}, f32[65,4096]{1,0:T(8,128)}, u32[]{:S(2)}, u32[]{:S(2)}) %collective-permute-start.1) | collective-permute-done | bytes 1064992 | tf_op jit(solution)/shard_map/ppermute | solution.py:12
  194.6 1.8 copy.68
  196.4 3.1 %slice_add_fusion = f32[65,4096]{0,1:T(8,128)} fusion(f32[65,4096]{0,1:T(8,128)S(1)} %copy.68, f32[65,8192]{0,1:T(8,128)} %scatter_custom_fusion), kind=kLoop, calls=%fused_computation.72 | loop fusion | flops 266240 | bytes 3194880 | tf_op jit(solution)/shard_map/add | solution.py:167
  199.6 78.8 %reduce-scatter.2.cloned.1.call-done = f32[65,256]{0,1:T(8,128)} async-done(((f32[65,4096]{0,1:T(8,128)}), f32[65,256]{0,1:T(8,128)}) %reduce-scatter.2.cloned.1.call-update) | async-done | bytes 66576 | tf_op jit(solution)/shard_map/reduce_scatter | solution.py:166
  278.4 1.6 copy.69
  280.0 1.7 slice_reduce_fusion
  (94 shorter events, 18.3 us)
Async XLA Ops:
  7.2 107.7 %copy-start = (bf16[64,512]{1,0:T(8,128)(2,1)S(1)}, bf16[64,512]{1,0:T(8,128)(2,1)}, u32[]{:S(2)}) copy-start(bf16[64,512]{1,0:T(8,128)(2,1)} %param.18) | copy-start | bytes 196612
  8.1 12.4 %collective-permute-start = (f32[69,256]{1,0:T(8,128)S(1)}, f32[69,256]{1,0:T(8,128)S(1)}, u32[]{:S(2)}, u32[]{:S(2)}) collective-permute-start(f32[69,256]{1,0:T(8,128)S(1)} %get-tuple-element.528), channel_id=1, source_target_pairs={{0,1},{1,2},{2,3},{3,4},{4,5},{5,6},{6,7},{7,8},{8,9},{9,10},{10,1... | collective-permute-start | bytes 211976 | tf_op jit(solution)/shard_map/ppermute | solution.py:12
  22.5 8.9 %copy-start.3 = (s32[1,1,16]{2,1,0:T(1,128)S(1)}, s32[1,1,16]{2,1,0:T(1,128)}, u32[]{:S(2)}) copy-start(s32[1,1,16]{2,1,0:T(1,128)} %param.20) | copy-start | bytes 196
  22.5 10.3 %copy-start.4 = (f32[16,3]{0,1:T(4,128)S(1)}, f32[16,3]{0,1:T(4,128)}, u32[]{:S(2)}) copy-start(f32[16,3]{0,1:T(4,128)} %param.17) | copy-start | bytes 580
  22.6 12.4 %copy-start.2 = (s32[1,1,16,256]{3,2,1,0:T(8,128)S(1)}, s32[1,1,16,256]{3,2,1,0:T(8,128)}, u32[]{:S(2)}) copy-start(s32[1,1,16,256]{3,2,1,0:T(8,128)} %param.19) | copy-start | bytes 49156
  22.6 55.0 %all-to-all-start = ((f32[16,2,69,256]{3,1,2,0:T(2,128)}), f32[16,2,69,256]{3,1,2,0:T(2,128)S(1)}, u32[]{:S(2)}, u32[]{:S(2)}) async-start(f32[16,2,69,256]{3,1,2,0:T(2,128)} %stack.11), calls=%async_computation | async-start | bytes 4521984 | tf_op jit(solution)/shard_map/all_to_all | solution.py:150
  31.4 247.0 %reduce-scatter.2.cloned.1.call-start = ((), (), s32[]{:S(2)}) async-start(), calls=%async_computation.2 | async-start | bytes 2228224 | tf_op jit(solution)/shard_map/reduce_scatter | solution.py:166
  114.9 2.2 copy-start.1
  173.2 1.6 slice-start
  175.7 18.9 %collective-permute-start.1 = (f32[65,4096]{1,0:T(8,128)S(1)}, f32[65,4096]{1,0:T(8,128)}, u32[]{:S(2)}, u32[]{:S(2)}) collective-permute-start(f32[65,4096]{1,0:T(8,128)S(1)} %copy.67), channel_id=1, source_target_pairs={{1,0},{2,1},{3,2},{4,3},{5,4},{6,5},{7,6},{8,7},{9,8},{10,9},{11,1... | collective-permute-start | bytes 3194888 | tf_op jit(solution)/shard_map/ppermute | solution.py:12
Sparse Core Ops, SparseCore 0:
  199.7 78.6 reduce-scatter.1
